TPU v7x, 256 devices: a whole 4x4x8 slice. The times are simulated.
256 devices in a mesh: tx: 16 (over z, core), gx: 8 (over x, y_lo), gy: 2 (over y_hi).
Axes of the slice: x: 4, y: 4 (y_hi: 2, y_lo: 2; y = y_hi * 2 + y_lo), z: 8, core: 2. Of those that a mesh axis runs over, the one named last changes fastest.
Arguments:
- cond_h: float32 [128, 32, 128], P('gx', 'gy'), may hold values from 0.1 to 1.5
- cond_v: float32 [128, 32, 128], P('gx', 'gy'), may hold values from 0.1 to 1.5
- fwd_init: float32 [16, 6, 128, 32, 128], P('tx', None, 'gx', 'gy'), may hold values from -6 to 6
- adj_init: float32 [16, 6, 128, 32, 128], P('tx', None, 'gx', 'gy'), may hold values from -6 to 6
- observed: float32 [16, 4, 8, 2, 2, 32], P('tx', None, 'gx', 'gy'), may hold values from -6 to 6
- footprint: int32 [16, 8, 2], P('tx', 'gx', 'gy'), may hold values 0 or 1
- owner: int32 [8, 2, 16], P('gx', 'gy'), may hold values from 0 to 15, each once within a row
- rec_cells: int32 [8, 2, 32], P('gx', 'gy'), may hold values from 0 to 255
Outputs:
- owned_gradient: float32 [8, 16, 2, 1, 32, 128], P('gx', 'tx', None, None, 'gy')
- misfit: float32 [], replicated
Inputs may be any that keep to these rules, and one draw needn't show every extreme that they name: `owner`: each tile's row is a permutation of 0 to 15. `rec_cells`: cell index x * 16 + y within the tile; receivers may share a cell. `footprint`: 1 where the group's gradient counts in the tile.
All inputs are finite; a program needn't handle non-finite values.
Results may differ from a plain program's by a relative error of at most 0.00028.
Values sent between devices are 32-bit elements; how exact they have to be, the bound alone decides.
No kernel may reach another device: no remote copies, remote signals or barrier semaphores. Data moves between devices by JAX's collectives and lax.ppermute only.
A program may use at most 64 MiB of HBM per device.

v0:
```python
import jax
import jax.numpy as jnp
from jax import lax
from jax.sharding import PartitionSpec as P

STEPS = 4
ZREC = 32
STEP_DT = 0.5


def shifted(x, axis, by):
    size = lax.axis_size(axis)
    pairs = [(i, i + by) for i in range(size) if 0 <= i + by < size]
    return lax.ppermute(x, axis, pairs)


def coefficients(conduct):
    half_rate = 0.25 * conduct
    return ((1.0 - half_rate) / (1.0 + half_rate), STEP_DT / (1.0 + half_rate))


def ahead_of(values, tail_plane, axis_num):
    extent = values.shape[axis_num]
    return jnp.concatenate(
        [lax.slice_in_dim(values, 1, extent, axis=axis_num), tail_plane], axis=axis_num
    )


def before(values, head_plane, axis_num):
    extent = values.shape[axis_num]
    return jnp.concatenate(
        [head_plane, lax.slice_in_dim(values, 0, extent - 1, axis=axis_num)], axis=axis_num
    )


def zero_plane(values, axis_num):
    return jnp.zeros_like(lax.slice_in_dim(values, 0, 1, axis=axis_num))


def curl_ahead(field, next_x, next_y):
    comp_x, comp_y, comp_z = (field[0], field[1], field[2])
    out_x = (
        ahead_of(comp_z, next_y[1], 1)
        - comp_z
        - (ahead_of(comp_y, zero_plane(comp_y, 2), 2) - comp_y)
    )
    out_y = (
        ahead_of(comp_x, zero_plane(comp_x, 2), 2)
        - comp_x
        - (ahead_of(comp_z, next_x[1], 0) - comp_z)
    )
    out_z = ahead_of(comp_y, next_x[0], 0) - comp_y - (ahead_of(comp_x, next_y[0], 1) - comp_x)
    return jnp.stack([out_x, out_y, out_z])


def curl_before(field, prev_x, prev_y):
    comp_x, comp_y, comp_z = (field[0], field[1], field[2])
    out_x = (
        comp_z - before(comp_z, prev_y[1], 1) - (comp_y - before(comp_y, zero_plane(comp_y, 2), 2))
    )
    out_y = (
        comp_x - before(comp_x, zero_plane(comp_x, 2), 2) - (comp_z - before(comp_z, prev_x[1], 0))
    )
    out_z = comp_y - before(comp_y, prev_x[0], 0) - (comp_x - before(comp_x, prev_y[0], 1))
    return jnp.stack([out_x, out_y, out_z])


def electric_rims(electric):
    next_x = shifted(electric[1:3, 0:1], "gx", -1)
    next_y = shifted(electric[0::2, :, 0:1], "gy", -1)
    return (next_x, next_y)


def magnetic_rims(magnetic):
    size_x = magnetic.shape[1]
    size_y = magnetic.shape[2]
    prev_x = shifted(magnetic[1:3, size_x - 1 : size_x], "gx", 1)
    prev_y = shifted(magnetic[0::2, :, size_y - 1 : size_y], "gy", 1)
    return (prev_x, prev_y)


def advance(electric, magnetic, decay, drive):
    next_x, next_y = electric_rims(electric)
    magnetic = magnetic - STEP_DT * curl_ahead(electric, next_x, next_y)
    prev_x, prev_y = magnetic_rims(magnetic)
    electric = decay * electric + drive * curl_before(magnetic, prev_x, prev_y)
    return (electric, magnetic)


def on_device(cond_h, cond_v, fwd_init, adj_init, observed, footprint, owner, rec_cells):
    size_x, size_y, depth = cond_h.shape
    decay_h, drive_h = coefficients(cond_h)
    decay_v, drive_v = coefficients(cond_v)
    highest = lax.Precision.HIGHEST
    cell_ids = jnp.arange(size_x * size_y, dtype=jnp.int32)
    onehot = (rec_cells[0, 0][:, None] == cell_ids[None, :]).astype(jnp.float32)
    observe = observed[0, :, 0, 0]
    grad_h = jnp.zeros((size_x, size_y, depth), jnp.float32)
    grad_v = jnp.zeros((size_x, size_y, depth), jnp.float32)
    residuals = []
    decay = jnp.stack([decay_h, decay_h, decay_v])
    drive = jnp.stack([drive_h, drive_h, drive_v])
    electric, magnetic = (fwd_init[0, 0:3], fwd_init[0, 3:6])
    stored = []
    for step_idx in range(STEPS):
        electric, magnetic = advance(electric, magnetic, decay, drive)
        stored.append(electric)
        planes = electric[0:2, :, :, ZREC].reshape(2, size_x * size_y)
        residuals.append(jnp.dot(planes, onehot.T, precision=highest) - observe[step_idx])
    adj_e, adj_h = (adj_init[0, 0:3], adj_init[0, 3:6])
    for step_idx in reversed(range(STEPS)):
        adj_e = adj_e.at[0:2, :, :, ZREC].add(
            jnp.dot(residuals[step_idx], onehot, precision=highest).reshape(2, size_x, size_y)
        )
        adj_e, adj_h = advance(adj_e, adj_h, decay, drive)
        kept = stored[step_idx]
        grad_h = grad_h + adj_e[0] * kept[0] + adj_e[1] * kept[1]
        grad_v = grad_v + adj_e[2] * kept[2]
    local_misfit = jnp.float32(0.0)
    for step_idx in range(STEPS):
        local_misfit = local_misfit + 0.5 * jnp.sum(residuals[step_idx] * residuals[step_idx])
    misfit = lax.psum(local_misfit, ("tx", "gx", "gy"))
    tile_flag = footprint[0, 0, 0].astype(jnp.float32)
    gradient = jnp.stack([grad_h, grad_v]) * tile_flag
    groups_count = lax.axis_size("tx")
    block_rows = size_x // groups_count
    blocked = gradient.reshape(2, groups_count, block_rows, size_y, depth)
    ordered = jnp.take(blocked, owner[0, 0], axis=1)
    summed = lax.psum_scatter(ordered, "tx", scatter_dimension=1, tiled=True)
    owned_part = summed.reshape(1, 1, 2, block_rows, size_y, depth)
    return (owned_part, misfit)


def solution(mesh):
    placed = (
        P("gx", "gy", None),
        P("gx", "gy", None),
        P("tx", None, "gx", "gy", None),
        P("tx", None, "gx", "gy", None),
        P("tx", None, "gx", "gy", None, None),
        P("tx", "gx", "gy"),
        P("gx", "gy", None),
        P("gx", "gy", None),
    )
    return jax.shard_map(
        on_device,
        mesh=mesh,
        in_specs=placed,
        out_specs=(P("gx", "tx", None, None, "gy", None), P()),
        check_vma=False,
    )
```

profile of v0, /device:TPU:1, one launch (start us, length us, event | category | flops | bytes accessed | tf_op | source)
XLA Modules:
  0.0 326.6 jit_solution(11279298193173657843)
XLA Ops:
  19.2 5.6 %collective-permute-start.2 = (f32[2,16,1,128]{3,1,2,0:T(8,128)S(1)}, f32[2,16,1,128]{3,1,2,0:T(8,128)S(1)}, u32[]{:S(2)}, u32[]{:S(2)}) collective-permute-start(f32[2,16,1,128]{3,1,2,0:T(8,128)S(1)} %bitcast.592), channel_id=1, source_target_pairs={{0,1},{2,3},{4,5},{6,7},{8,9},{10,11},{12,13},{14,15},{16,17},{18,... | collective-permute-start | bytes 49160 | tf_op jit(solution)/shard_map/ppermute | solution.py:14
  24.9 4.5 %collective-permute-start.3 = (f32[2,1,16,128]{3,2,1,0:T(8,128)S(1)}, f32[2,1,16,128]{3,2,1,0:T(8,128)S(1)}, u32[]{:S(2)}, u32[]{:S(2)}) collective-permute-start(f32[2,1,16,128]{3,2,1,0:T(8,128)S(1)} %slice.1340), channel_id=1, source_target_pairs={{0,2},{2,4},{4,6},{6,8},{8,10},{10,12},{12,14},{1,3},{3,5},{5,7},{... | collective-permute-start | bytes 49160 | tf_op jit(solution)/shard_map/ppermute | solution.py:14
  41.6 6.1 %collective-permute-start.6 = (f32[2,16,1,128]{3,1,2,0:T(8,128)S(1)}, f32[2,16,1,128]{3,1,2,0:T(8,128)S(1)}, u32[]{:S(2)}, u32[]{:S(2)}) collective-permute-start(f32[2,16,1,128]{3,1,2,0:T(8,128)S(1)} %bitcast.593), channel_id=1, source_target_pairs={{0,1},{2,3},{4,5},{6,7},{8,9},{10,11},{12,13},{14,15},{16,17},{18,... | collective-permute-start | bytes 49160 | tf_op jit(solution)/shard_map/ppermute | solution.py:14
  47.8 3.7 %collective-permute-start.7 = (f32[2,1,16,128]{3,2,1,0:T(8,128)S(1)}, f32[2,1,16,128]{3,2,1,0:T(8,128)S(1)}, u32[]{:S(2)}, u32[]{:S(2)}) collective-permute-start(f32[2,1,16,128]{3,2,1,0:T(8,128)S(1)} %slice.1368), channel_id=1, source_target_pairs={{0,2},{2,4},{4,6},{6,8},{8,10},{10,12},{12,14},{1,3},{3,5},{5,7},{... | collective-permute-start | bytes 49160 | tf_op jit(solution)/shard_map/ppermute | solution.py:14
  68.3 6.1 %collective-permute-start.10 = (f32[2,16,1,128]{3,1,2,0:T(8,128)S(1)}, f32[2,16,1,128]{3,1,2,0:T(8,128)S(1)}, u32[]{:S(2)}, u32[]{:S(2)}) collective-permute-start(f32[2,16,1,128]{3,1,2,0:T(8,128)S(1)} %bitcast.594), channel_id=1, source_target_pairs={{0,1},{2,3},{4,5},{6,7},{8,9},{10,11},{12,13},{14,15},{16,17},{18,... | collective-permute-start | bytes 49160 | tf_op jit(solution)/shard_map/ppermute | solution.py:14
  74.5 3.7 %collective-permute-start.11 = (f32[2,1,16,128]{3,2,1,0:T(8,128)S(1)}, f32[2,1,16,128]{3,2,1,0:T(8,128)S(1)}, u32[]{:S(2)}, u32[]{:S(2)}) collective-permute-start(f32[2,1,16,128]{3,2,1,0:T(8,128)S(1)} %slice.1396), channel_id=1, source_target_pairs={{0,2},{2,4},{4,6},{6,8},{8,10},{10,12},{12,14},{1,3},{3,5},{5,7},{... | collective-permute-start | bytes 49160 | tf_op jit(solution)/shard_map/ppermute | solution.py:14
  97.4 5.9 %collective-permute-start.14 = (f32[2,16,1,128]{3,1,2,0:T(8,128)S(1)}, f32[2,16,1,128]{3,1,2,0:T(8,128)S(1)}, u32[]{:S(2)}, u32[]{:S(2)}) collective-permute-start(f32[2,16,1,128]{3,1,2,0:T(8,128)S(1)} %bitcast.595), channel_id=1, source_target_pairs={{0,1},{2,3},{4,5},{6,7},{8,9},{10,11},{12,13},{14,15},{16,17},{18,... | collective-permute-start | bytes 49160 | tf_op jit(solution)/shard_map/ppermute | solution.py:14
  103.3 3.7 %collective-permute-start.15 = (f32[2,1,16,128]{3,2,1,0:T(8,128)S(1)}, f32[2,1,16,128]{3,2,1,0:T(8,128)S(1)}, u32[]{:S(2)}, u32[]{:S(2)}) collective-permute-start(f32[2,1,16,128]{3,2,1,0:T(8,128)S(1)} %slice.1424), channel_id=1, source_target_pairs={{0,2},{2,4},{4,6},{6,8},{8,10},{10,12},{12,14},{1,3},{3,5},{5,7},{... | collective-permute-start | bytes 49160 | tf_op jit(solution)/shard_map/ppermute | solution.py:14
  114.3 3.6 %scatter-add.14 = f32[3,16,16,128]{3,2,1,0:T(8,128)S(1)} dynamic-update-slice(f32[3,16,16,128]{3,2,1,0:T(8,128)S(1)} %get-tuple-element.51, f32[2,16,16,1]{3,2,1,0:T(8,128)S(1)} %add_select_fusion.3, s32[]{:T(128)} %bitcast.4, s32[]{:T(128)} %constant.106.clone.1, s32[]{:T(128)} %constant.106.clone.1, s32[]{:T(128)} %bitcast.5) | dynamic-update-slice | bytes 4100 | tf_op jit(solution)/shard_map/scatter-add | solution.py:112
  120.7 3.3 collective-permute-done.16
  126.3 6.1 %collective-permute-start.18 = (f32[2,16,1,128]{3,1,2,0:T(8,128)S(1)}, f32[2,16,1,128]{3,1,2,0:T(8,128)S(1)}, u32[]{:S(2)}, u32[]{:S(2)}) collective-permute-start(f32[2,16,1,128]{3,1,2,0:T(8,128)S(1)} %bitcast.596), channel_id=1, source_target_pairs={{0,1},{2,3},{4,5},{6,7},{8,9},{10,11},{12,13},{14,15},{16,17},{18,... | collective-permute-start | bytes 49160 | tf_op jit(solution)/shard_map/ppermute | solution.py:14
  132.4 3.7 %collective-permute-start.19 = (f32[2,1,16,128]{3,2,1,0:T(8,128)S(1)}, f32[2,1,16,128]{3,2,1,0:T(8,128)S(1)}, u32[]{:S(2)}, u32[]{:S(2)}) collective-permute-start(f32[2,1,16,128]{3,2,1,0:T(8,128)S(1)} %slice.1453), channel_id=1, source_target_pairs={{0,2},{2,4},{4,6},{6,8},{8,10},{10,12},{12,14},{1,3},{3,5},{5,7},{... | collective-permute-start | bytes 49160 | tf_op jit(solution)/shard_map/ppermute | solution.py:14
  140.3 3.6 %scatter-add.15 = f32[3,16,16,128]{3,2,1,0:T(8,128)S(1)} dynamic-update-slice(f32[3,16,16,128]{3,2,1,0:T(8,128)S(1)} %copy.87, f32[2,16,16,1]{3,2,1,0:T(8,128)S(1)} %add_select_fusion.2, s32[]{:T(128)} %bitcast.4, s32[]{:T(128)} %constant.106.clone.1, s32[]{:T(128)} %constant.106.clone.1, s32[]{:T(128)} %bitcast.5) | dynamic-update-slice | bytes 4100 | tf_op jit(solution)/shard_map/scatter-add | solution.py:112
  146.7 3.3 collective-permute-done.20
  151.7 6.1 %collective-permute-start.22 = (f32[2,16,1,128]{3,1,2,0:T(8,128)S(1)}, f32[2,16,1,128]{3,1,2,0:T(8,128)S(1)}, u32[]{:S(2)}, u32[]{:S(2)}) collective-permute-start(f32[2,16,1,128]{3,1,2,0:T(8,128)S(1)} %bitcast.597), channel_id=1, source_target_pairs={{0,1},{2,3},{4,5},{6,7},{8,9},{10,11},{12,13},{14,15},{16,17},{18,... | collective-permute-start | bytes 49160 | tf_op jit(solution)/shard_map/ppermute | solution.py:14
  157.8 3.7 %collective-permute-start.23 = (f32[2,1,16,128]{3,2,1,0:T(8,128)S(1)}, f32[2,1,16,128]{3,2,1,0:T(8,128)S(1)}, u32[]{:S(2)}, u32[]{:S(2)}) collective-permute-start(f32[2,1,16,128]{3,2,1,0:T(8,128)S(1)} %slice.1486), channel_id=1, source_target_pairs={{0,2},{2,4},{4,6},{6,8},{8,10},{10,12},{12,14},{1,3},{3,5},{5,7},{... | collective-permute-start | bytes 49160 | tf_op jit(solution)/shard_map/ppermute | solution.py:14
  165.6 3.6 %scatter-add.16 = f32[3,16,16,128]{3,2,1,0:T(8,128)S(1)} dynamic-update-slice(f32[3,16,16,128]{3,2,1,0:T(8,128)S(1)} %copy.88, f32[2,16,16,1]{3,2,1,0:T(8,128)S(1)} %add_select_fusion.1, s32[]{:T(128)} %bitcast.4, s32[]{:T(128)} %constant.106.clone.1, s32[]{:T(128)} %constant.106.clone.1, s32[]{:T(128)} %bitcast.5) | dynamic-update-slice | bytes 4100 | tf_op jit(solution)/shard_map/scatter-add | solution.py:112
  177.5 6.1 %collective-permute-start.26 = (f32[2,16,1,128]{3,1,2,0:T(8,128)S(1)}, f32[2,16,1,128]{3,1,2,0:T(8,128)S(1)}, u32[]{:S(2)}, u32[]{:S(2)}) collective-permute-start(f32[2,16,1,128]{3,1,2,0:T(8,128)S(1)} %bitcast.598), channel_id=1, source_target_pairs={{0,1},{2,3},{4,5},{6,7},{8,9},{10,11},{12,13},{14,15},{16,17},{18,... | collective-permute-start | bytes 49160 | tf_op jit(solution)/shard_map/ppermute | solution.py:14
  183.6 3.7 %collective-permute-start.27 = (f32[2,1,16,128]{3,2,1,0:T(8,128)S(1)}, f32[2,1,16,128]{3,2,1,0:T(8,128)S(1)}, u32[]{:S(2)}, u32[]{:S(2)}) collective-permute-start(f32[2,1,16,128]{3,2,1,0:T(8,128)S(1)} %slice.1517), channel_id=1, source_target_pairs={{0,2},{2,4},{4,6},{6,8},{8,10},{10,12},{12,14},{1,3},{3,5},{5,7},{... | collective-permute-start | bytes 49160 | tf_op jit(solution)/shard_map/ppermute | solution.py:14
  191.6 3.6 %scatter-add.19 = f32[3,16,16,128]{3,2,1,0:T(8,128)S(1)} dynamic-update-slice(f32[3,16,16,128]{3,2,1,0:T(8,128)S(1)} %copy.89, f32[2,16,16,1]{3,2,1,0:T(8,128)S(1)} %add_select_fusion, s32[]{:T(128)} %bitcast.4, s32[]{:T(128)} %constant.106.clone.1, s32[]{:T(128)} %constant.106.clone.1, s32[]{:T(128)} %bitcast.5) | dynamic-update-slice | bytes 4100 | tf_op jit(solution)/shard_map/scatter-add | solution.py:112
  198.0 3.3 collective-permute-done.28
  203.1 6.1 %collective-permute-start.30 = (f32[2,16,1,128]{3,1,2,0:T(8,128)S(1)}, f32[2,16,1,128]{3,1,2,0:T(8,128)S(1)}, u32[]{:S(2)}, u32[]{:S(2)}) collective-permute-start(f32[2,16,1,128]{3,1,2,0:T(8,128)S(1)} %bitcast.599), channel_id=1, source_target_pairs={{0,1},{2,3},{4,5},{6,7},{8,9},{10,11},{12,13},{14,15},{16,17},{18,... | collective-permute-start | bytes 49160 | tf_op jit(solution)/shard_map/ppermute | solution.py:14
  209.3 3.7 %collective-permute-start.31 = (f32[2,1,16,128]{3,2,1,0:T(8,128)S(1)}, f32[2,1,16,128]{3,2,1,0:T(8,128)S(1)}, u32[]{:S(2)}, u32[]{:S(2)}) collective-permute-start(f32[2,1,16,128]{3,2,1,0:T(8,128)S(1)} %slice.1548), channel_id=1, source_target_pairs={{0,2},{2,4},{4,6},{6,8},{8,10},{10,12},{12,14},{1,3},{3,5},{5,7},{... | collective-permute-start | bytes 49160 | tf_op jit(solution)/shard_map/ppermute | solution.py:14
  219.5 100.3 %psum.7 = f32[]{:T(128)} all-reduce(f32[]{:T(128)S(6)} %add.229), channel_id=1, replica_groups=mesh['tx'=16,'gx'=8,'gy'=2] {'tx','gx','gy'}, use_global_device_ids=true, to_apply=%region_6.0 | all-reduce | flops 1 | bytes 8 | tf_op jit(solution)/shard_map/psum | solution.py:122
  (437 shorter events, 104.6 us)
Async XLA Ops:
  7.2 312.6 %reduce-scatter.2.cloned.1.call-start = ((), (), s32[]{:S(2)}) async-start(), calls=%async_computation.1 | async-start | bytes 278528 | tf_op jit(solution)/shard_map/reduce_scatter | solution.py:129
  8.3 10.5 %collective-permute-start = (f32[2,16,1,128]{3,2,1,0:T(1,128)S(1)}, f32[2,16,1,128]{3,2,1,0:T(1,128)S(1)}, u32[]{:S(2)}, u32[]{:S(2)}) collective-permute-start(f32[2,16,1,128]{3,2,1,0:T(1,128)S(1)} %slice.1044), channel_id=1, source_target_pairs={{1,0},{3,2},{5,4},{7,6},{9,8},{11,10},{13,12},{15,14},{17,16},{19,... | collective-permute-start | bytes 49160 | tf_op jit(solution)/shard_map/ppermute | solution.py:14
  9.6 9.2 %collective-permute-start.1 = (f32[2,1,16,128]{3,2,1,0:T(8,128)S(1)}, f32[2,1,16,128]{3,2,1,0:T(8,128)S(1)}, u32[]{:S(2)}, u32[]{:S(2)}) collective-permute-start(f32[2,1,16,128]{3,2,1,0:T(8,128)S(1)} %slice.1328), channel_id=1, source_target_pairs={{2,0},{4,2},{6,4},{8,6},{10,8},{12,10},{14,12},{3,1},{5,3},{7,5},{... | collective-permute-start | bytes 49160 | tf_op jit(solution)/shard_map/ppermute | solution.py:14
  19.2 10.2 %collective-permute-start.2 = (f32[2,16,1,128]{3,1,2,0:T(8,128)S(1)}, f32[2,16,1,128]{3,1,2,0:T(8,128)S(1)}, u32[]{:S(2)}, u32[]{:S(2)}) collective-permute-start(f32[2,16,1,128]{3,1,2,0:T(8,128)S(1)} %bitcast.592), channel_id=1, source_target_pairs={{0,1},{2,3},{4,5},{6,7},{8,9},{10,11},{12,13},{14,15},{16,17},{18,... | collective-permute-start | bytes 49160 | tf_op jit(solution)/shard_map/ppermute | solution.py:14
  24.9 5.4 %collective-permute-start.3 = (f32[2,1,16,128]{3,2,1,0:T(8,128)S(1)}, f32[2,1,16,128]{3,2,1,0:T(8,128)S(1)}, u32[]{:S(2)}, u32[]{:S(2)}) collective-permute-start(f32[2,1,16,128]{3,2,1,0:T(8,128)S(1)} %slice.1340), channel_id=1, source_target_pairs={{0,2},{2,4},{4,6},{6,8},{8,10},{10,12},{12,14},{1,3},{3,5},{5,7},{... | collective-permute-start | bytes 49160 | tf_op jit(solution)/shard_map/ppermute | solution.py:14
  32.5 6.0 %collective-permute-start.4 = (f32[2,16,1,128]{3,2,1,0:T(1,128)S(1)}, f32[2,16,1,128]{3,2,1,0:T(1,128)S(1)}, u32[]{:S(2)}, u32[]{:S(2)}) collective-permute-start(f32[2,16,1,128]{3,2,1,0:T(1,128)S(1)} %slice.1076), channel_id=1, source_target_pairs={{1,0},{3,2},{5,4},{7,6},{9,8},{11,10},{13,12},{15,14},{17,16},{19,... | collective-permute-start | bytes 49160 | tf_op jit(solution)/shard_map/ppermute | solution.py:14
  33.8 6.0 %collective-permute-start.5 = (f32[2,1,16,128]{3,2,1,0:T(8,128)S(1)}, f32[2,1,16,128]{3,2,1,0:T(8,128)S(1)}, u32[]{:S(2)}, u32[]{:S(2)}) collective-permute-start(f32[2,1,16,128]{3,2,1,0:T(8,128)S(1)} %slice.1355), channel_id=1, source_target_pairs={{2,0},{4,2},{6,4},{8,6},{10,8},{12,10},{14,12},{3,1},{5,3},{7,5},{... | collective-permute-start | bytes 49160 | tf_op jit(solution)/shard_map/ppermute | solution.py:14
  41.6 9.8 %collective-permute-start.6 = (f32[2,16,1,128]{3,1,2,0:T(8,128)S(1)}, f32[2,16,1,128]{3,1,2,0:T(8,128)S(1)}, u32[]{:S(2)}, u32[]{:S(2)}) collective-permute-start(f32[2,16,1,128]{3,1,2,0:T(8,128)S(1)} %bitcast.593), channel_id=1, source_target_pairs={{0,1},{2,3},{4,5},{6,7},{8,9},{10,11},{12,13},{14,15},{16,17},{18,... | collective-permute-start | bytes 49160 | tf_op jit(solution)/shard_map/ppermute | solution.py:14
  57.8 6.0 %collective-permute-start.8 = (f32[2,16,1,128]{3,2,1,0:T(1,128)S(1)}, f32[2,16,1,128]{3,2,1,0:T(1,128)S(1)}, u32[]{:S(2)}, u32[]{:S(2)}) collective-permute-start(f32[2,16,1,128]{3,2,1,0:T(1,128)S(1)} %copy-done.74), channel_id=1, source_target_pairs={{1,0},{3,2},{5,4},{7,6},{9,8},{11,10},{13,12},{15,14},{17,16},{19,... | collective-permute-start | bytes 49160 | tf_op jit(solution)/shard_map/ppermute | solution.py:14
  59.1 5.9 %collective-permute-start.9 = (f32[2,1,16,128]{3,2,1,0:T(8,128)S(1)}, f32[2,1,16,128]{3,2,1,0:T(8,128)S(1)}, u32[]{:S(2)}, u32[]{:S(2)}) collective-permute-start(f32[2,1,16,128]{3,2,1,0:T(8,128)S(1)} %copy-done.72), channel_id=1, source_target_pairs={{2,0},{4,2},{6,4},{8,6},{10,8},{12,10},{14,12},{3,1},{5,3},{7,5},{... | collective-permute-start | bytes 49160 | tf_op jit(solution)/shard_map/ppermute | solution.py:14
  68.3 9.8 %collective-permute-start.10 = (f32[2,16,1,128]{3,1,2,0:T(8,128)S(1)}, f32[2,16,1,128]{3,1,2,0:T(8,128)S(1)}, u32[]{:S(2)}, u32[]{:S(2)}) collective-permute-start(f32[2,16,1,128]{3,1,2,0:T(8,128)S(1)} %bitcast.594), channel_id=1, source_target_pairs={{0,1},{2,3},{4,5},{6,7},{8,9},{10,11},{12,13},{14,15},{16,17},{18,... | collective-permute-start | bytes 49160 | tf_op jit(solution)/shard_map/ppermute | solution.py:14
  86.1 6.4 %collective-permute-start.12 = (f32[2,16,1,128]{3,1,2,0:T(8,128)}, f32[2,16,1,128]{3,1,2,0:T(8,128)}, u32[]{:S(2)}, u32[]{:S(2)}) collective-permute-start(f32[2,16,1,128]{3,1,2,0:T(8,128)} %bitcast.197), channel_id=1, source_target_pairs={{1,0},{3,2},{5,4},{7,6},{9,8},{11,10},{13,12},{15,14},{17,16},{19,... | collective-permute-start | bytes 49160 | tf_op jit(solution)/shard_map/ppermute | solution.py:14
  87.5 5.7 %collective-permute-start.13 = (f32[2,1,16,128]{3,2,1,0:T(8,128)S(1)}, f32[2,1,16,128]{3,2,1,0:T(8,128)}, u32[]{:S(2)}, u32[]{:S(2)}) collective-permute-start(f32[2,1,16,128]{3,2,1,0:T(8,128)S(1)} %copy-done.73), channel_id=1, source_target_pairs={{2,0},{4,2},{6,4},{8,6},{10,8},{12,10},{14,12},{3,1},{5,3},{7,5},{... | collective-permute-start | bytes 49160 | tf_op jit(solution)/shard_map/ppermute | solution.py:14
  97.4 9.6 %collective-permute-start.14 = (f32[2,16,1,128]{3,1,2,0:T(8,128)S(1)}, f32[2,16,1,128]{3,1,2,0:T(8,128)S(1)}, u32[]{:S(2)}, u32[]{:S(2)}) collective-permute-start(f32[2,16,1,128]{3,1,2,0:T(8,128)S(1)} %bitcast.595), channel_id=1, source_target_pairs={{0,1},{2,3},{4,5},{6,7},{8,9},{10,11},{12,13},{14,15},{16,17},{18,... | collective-permute-start | bytes 49160 | tf_op jit(solution)/shard_map/ppermute | solution.py:14
  118.0 6.0 %collective-permute-start.16 = (f32[2,16,1,128]{3,1,2,0:T(8,128)S(1)}, f32[2,16,1,128]{3,1,2,0:T(8,128)S(1)}, u32[]{:S(2)}, u32[]{:S(2)}) collective-permute-start(f32[2,16,1,128]{3,1,2,0:T(8,128)S(1)} %bitcast.589), channel_id=1, source_target_pairs={{1,0},{3,2},{5,4},{7,6},{9,8},{11,10},{13,12},{15,14},{17,16},{19,... | collective-permute-start | bytes 49160 | tf_op jit(solution)/shard_map/ppermute | solution.py:14
  119.4 5.5 %collective-permute-start.17 = (f32[2,1,16,128]{3,2,1,0:T(8,128)S(1)}, f32[2,1,16,128]{3,2,1,0:T(8,128)S(1)}, u32[]{:S(2)}, u32[]{:S(2)}) collective-permute-start(f32[2,1,16,128]{3,2,1,0:T(8,128)S(1)} %slice.1440), channel_id=1, source_target_pairs={{2,0},{4,2},{6,4},{8,6},{10,8},{12,10},{14,12},{3,1},{5,3},{7,5},{... | collective-permute-start | bytes 49160 | tf_op jit(solution)/shard_map/ppermute | solution.py:14
  126.3 9.8 %collective-permute-start.18 = (f32[2,16,1,128]{3,1,2,0:T(8,128)S(1)}, f32[2,16,1,128]{3,1,2,0:T(8,128)S(1)}, u32[]{:S(2)}, u32[]{:S(2)}) collective-permute-start(f32[2,16,1,128]{3,1,2,0:T(8,128)S(1)} %bitcast.596), channel_id=1, source_target_pairs={{0,1},{2,3},{4,5},{6,7},{8,9},{10,11},{12,13},{14,15},{16,17},{18,... | collective-permute-start | bytes 49160 | tf_op jit(solution)/shard_map/ppermute | solution.py:14
  143.9 6.0 %collective-permute-start.20 = (f32[2,16,1,128]{3,1,2,0:T(8,128)S(1)}, f32[2,16,1,128]{3,1,2,0:T(8,128)S(1)}, u32[]{:S(2)}, u32[]{:S(2)}) collective-permute-start(f32[2,16,1,128]{3,1,2,0:T(8,128)S(1)} %bitcast.590), channel_id=1, source_target_pairs={{1,0},{3,2},{5,4},{7,6},{9,8},{11,10},{13,12},{15,14},{17,16},{19,... | collective-permute-start | bytes 49160 | tf_op jit(solution)/shard_map/ppermute | solution.py:14
  151.7 9.8 %collective-permute-start.22 = (f32[2,16,1,128]{3,1,2,0:T(8,128)S(1)}, f32[2,16,1,128]{3,1,2,0:T(8,128)S(1)}, u32[]{:S(2)}, u32[]{:S(2)}) collective-permute-start(f32[2,16,1,128]{3,1,2,0:T(8,128)S(1)} %bitcast.597), channel_id=1, source_target_pairs={{0,1},{2,3},{4,5},{6,7},{8,9},{10,11},{12,13},{14,15},{16,17},{18,... | collective-permute-start | bytes 49160 | tf_op jit(solution)/shard_map/ppermute | solution.py:14
  169.3 6.0 %collective-permute-start.24 = (f32[2,16,1,128]{3,1,2,0:T(8,128)S(1)}, f32[2,16,1,128]{3,1,2,0:T(8,128)S(1)}, u32[]{:S(2)}, u32[]{:S(2)}) collective-permute-start(f32[2,16,1,128]{3,1,2,0:T(8,128)S(1)} %bitcast.591), channel_id=1, source_target_pairs={{1,0},{3,2},{5,4},{7,6},{9,8},{11,10},{13,12},{15,14},{17,16},{19,... | collective-permute-start | bytes 49160 | tf_op jit(solution)/shard_map/ppermute | solution.py:14
  170.7 5.0 %collective-permute-start.25 = (f32[2,1,16,128]{3,2,1,0:T(8,128)S(1)}, f32[2,1,16,128]{3,2,1,0:T(8,128)S(1)}, u32[]{:S(2)}, u32[]{:S(2)}) collective-permute-start(f32[2,1,16,128]{3,2,1,0:T(8,128)S(1)} %slice.1504), channel_id=1, source_target_pairs={{2,0},{4,2},{6,4},{8,6},{10,8},{12,10},{14,12},{3,1},{5,3},{7,5},{... | collective-permute-start | bytes 49160 | tf_op jit(solution)/shard_map/ppermute | solution.py:14
  177.5 9.8 %collective-permute-start.26 = (f32[2,16,1,128]{3,1,2,0:T(8,128)S(1)}, f32[2,16,1,128]{3,1,2,0:T(8,128)S(1)}, u32[]{:S(2)}, u32[]{:S(2)}) collective-permute-start(f32[2,16,1,128]{3,1,2,0:T(8,128)S(1)} %bitcast.598), channel_id=1, source_target_pairs={{0,1},{2,3},{4,5},{6,7},{8,9},{10,11},{12,13},{14,15},{16,17},{18,... | collective-permute-start | bytes 49160 | tf_op jit(solution)/shard_map/ppermute | solution.py:14
  195.3 6.0 %collective-permute-start.28 = (f32[2,16,1,128]{3,2,1,0:T(1,128)S(1)}, f32[2,16,1,128]{3,2,1,0:T(1,128)S(1)}, u32[]{:S(2)}, u32[]{:S(2)}) collective-permute-start(f32[2,16,1,128]{3,2,1,0:T(1,128)S(1)} %slice.1285), channel_id=1, source_target_pairs={{1,0},{3,2},{5,4},{7,6},{9,8},{11,10},{13,12},{15,14},{17,16},{19,... | collective-permute-start | bytes 49160 | tf_op jit(solution)/shard_map/ppermute | solution.py:14
  203.1 9.8 %collective-permute-start.30 = (f32[2,16,1,128]{3,1,2,0:T(8,128)S(1)}, f32[2,16,1,128]{3,1,2,0:T(8,128)S(1)}, u32[]{:S(2)}, u32[]{:S(2)}) collective-permute-start(f32[2,16,1,128]{3,1,2,0:T(8,128)S(1)} %bitcast.599), channel_id=1, source_target_pairs={{0,1},{2,3},{4,5},{6,7},{8,9},{10,11},{12,13},{14,15},{16,17},{18,... | collective-permute-start | bytes 49160 | tf_op jit(solution)/shard_map/ppermute | solution.py:14
  (91 other events, 157.7 us)
Sparse Core Ops, SparseCore 0:
  217.1 75.4 reduce-scatter.1
where the time goes:
time: 329 us; the launch traced here: 327 us
  blocking collectives  100 us (30%)
  starting transfers between devices  99.3 us (30%)
  local copies, waits for them, and re-layouts  54.1 us (16%)
  waiting for transfers between devices  27.5 us (8%)
  between operations  19.4 us (6%)
  other arithmetic  18.6 us (6%)
  matrix products  7.47 us (2%)
    psum x1, blocking collectives, on_device(): misfit = lax.psum(local_misfit, ('tx', 'gx', 'gy'))  100 us
    ppermute x32, starting transfers between devices, shifted(): return lax.ppermute(x, axis, pairs)  99.2 us
    ppermute x32, waiting for transfers between devices, shifted(): return lax.ppermute(x, axis, pairs)  27.5 us
    unnamed x167, local copies, waits for them, and re-layouts  21.2 us
    scatter-add x4, local copies, waits for them, and re-layouts, on_device(): adj_e.at[0:2, :, :, ZREC]  14.4 us
    another operation x6, other arithmetic  10.1 us
  transfers between devices with their start and end apart: 33, of which 20 were waited for; matrix products, arithmetic and copies ran while one was open for 4% of the time, Pallas kernels for 0%

commit v1 on v0

--- a/solution.py
+++ b/solution.py
@@ -119,7 +119,8 @@
     local_misfit = jnp.float32(0.0)
     for step_idx in range(STEPS):
         local_misfit = local_misfit + 0.5 * jnp.sum(residuals[step_idx] * residuals[step_idx])
-    misfit = lax.psum(local_misfit, ("tx", "gx", "gy"))
+    value_now = lax.psum(local_misfit, "tx")
+    misfit = lax.psum(value_now, ("gx", "gy"))
     tile_flag = footprint[0, 0, 0].astype(jnp.float32)
     gradient = jnp.stack([grad_h, grad_v]) * tile_flag
     groups_count = lax.axis_size("tx")

time: 329 us -> 314 us (0.954)
  the two profiles are of different devices: /device:TPU:1 before, /device:TPU:16 now
where the time goes in v1:
time: 314 us; the launch traced here: 312 us
  starting transfers between devices  102 us (32%)
  blocking collectives  67.3 us (21%)
  local copies, waits for them, and re-layouts  56 us (18%)
  waiting for transfers between devices  40.3 us (13%)
  other arithmetic  19.8 us (6%)
  between operations  19.3 us (6%)
  matrix products  7.44 us (2%)
    ppermute x32, starting transfers between devices, shifted(): return lax.ppermute(x, axis, pairs)  102 us
    psum x1, blocking collectives, on_device(): misfit = lax.psum(value_now, ('gx', 'gy'))  41.1 us
    ppermute x32, waiting for transfers between devices, shifted(): return lax.ppermute(x, axis, pairs)  40.2 us
    psum x1, blocking collectives, on_device(): value_now = lax.psum(local_misfit, 'tx')  26.3 us
    unnamed x167, local copies, waits for them, and re-layouts  21.2 us
    scatter-add x4, local copies, waits for them, and re-layouts, on_device(): adj_e.at[0:2, :, :, ZREC]  16.3 us
    another operation x6, other arithmetic  11.3 us
  transfers between devices with their start and end apart: 33, of which 23 were waited for; matrix products, arithmetic and copies ran while one was open for 4% of the time, Pallas kernels for 0%

profile of v1, /device:TPU:16, one launch (start us, length us, event | category | flops | bytes accessed | tf_op | source)
XLA Modules:
  0.0 312.1 jit_solution(15283104082053208149)
XLA Ops:
  23.2 4.5 %collective-permute-start.3 = (f32[2,1,16,128]{3,2,1,0:T(8,128)S(1)}, f32[2,1,16,128]{3,2,1,0:T(8,128)S(1)}, u32[]{:S(2)}, u32[]{:S(2)}) collective-permute-start(f32[2,1,16,128]{3,2,1,0:T(8,128)S(1)} %slice.1340), channel_id=1, source_target_pairs={{0,2},{2,4},{4,6},{6,8},{8,10},{10,12},{12,14},{1,3},{3,5},{5,7},{... | collective-permute-start | bytes 49160 | tf_op jit(solution)/shard_map/ppermute | solution.py:14
  31.4 5.4 %collective-permute-start.4 = (f32[2,16,1,128]{3,2,1,0:T(1,128)S(1)}, f32[2,16,1,128]{3,2,1,0:T(1,128)S(1)}, u32[]{:S(2)}, u32[]{:S(2)}) collective-permute-start(f32[2,16,1,128]{3,2,1,0:T(1,128)S(1)} %slice.1076), channel_id=1, source_target_pairs={{1,0},{3,2},{5,4},{7,6},{9,8},{11,10},{13,12},{15,14},{17,16},{19,... | collective-permute-start | bytes 49160 | tf_op jit(solution)/shard_map/ppermute | solution.py:14
  46.6 4.8 %collective-permute-start.7 = (f32[2,1,16,128]{3,2,1,0:T(8,128)S(1)}, f32[2,1,16,128]{3,2,1,0:T(8,128)S(1)}, u32[]{:S(2)}, u32[]{:S(2)}) collective-permute-start(f32[2,1,16,128]{3,2,1,0:T(8,128)S(1)} %slice.1368), channel_id=1, source_target_pairs={{0,2},{2,4},{4,6},{6,8},{8,10},{10,12},{12,14},{1,3},{3,5},{5,7},{... | collective-permute-start | bytes 49160 | tf_op jit(solution)/shard_map/ppermute | solution.py:14
  58.3 5.4 %collective-permute-start.8 = (f32[2,16,1,128]{3,2,1,0:T(1,128)S(1)}, f32[2,16,1,128]{3,2,1,0:T(1,128)S(1)}, u32[]{:S(2)}, u32[]{:S(2)}) collective-permute-start(f32[2,16,1,128]{3,2,1,0:T(1,128)S(1)} %copy-done.74), channel_id=1, source_target_pairs={{1,0},{3,2},{5,4},{7,6},{9,8},{11,10},{13,12},{15,14},{17,16},{19,... | collective-permute-start | bytes 49160 | tf_op jit(solution)/shard_map/ppermute | solution.py:14
  66.2 4.1 %collective-permute-done.9 = f32[2,1,16,128]{3,2,1,0:T(8,128)S(1)} collective-permute-done((f32[2,1,16,128]{3,2,1,0:T(8,128)S(1)}, f32[2,1,16,128]{3,2,1,0:T(8,128)S(1)}, u32[]{:S(2)}, u32[]{:S(2)}) %collective-permute-start.9) | collective-permute-done | bytes 16416 | tf_op jit(solution)/shard_map/ppermute | solution.py:14
  74.9 4.8 %collective-permute-start.11 = (f32[2,1,16,128]{3,2,1,0:T(8,128)S(1)}, f32[2,1,16,128]{3,2,1,0:T(8,128)S(1)}, u32[]{:S(2)}, u32[]{:S(2)}) collective-permute-start(f32[2,1,16,128]{3,2,1,0:T(8,128)S(1)} %slice.1396), channel_id=1, source_target_pairs={{0,2},{2,4},{4,6},{6,8},{8,10},{10,12},{12,14},{1,3},{3,5},{5,7},{... | collective-permute-start | bytes 49160 | tf_op jit(solution)/shard_map/ppermute | solution.py:14
  88.3 6.2 %collective-permute-start.12 = (f32[2,16,1,128]{3,1,2,0:T(8,128)}, f32[2,16,1,128]{3,1,2,0:T(8,128)}, u32[]{:S(2)}, u32[]{:S(2)}) collective-permute-start(f32[2,16,1,128]{3,1,2,0:T(8,128)} %bitcast.197), channel_id=1, source_target_pairs={{1,0},{3,2},{5,4},{7,6},{9,8},{11,10},{13,12},{15,14},{17,16},{19,... | collective-permute-start | bytes 49160 | tf_op jit(solution)/shard_map/ppermute | solution.py:14
  106.6 4.8 %collective-permute-start.15 = (f32[2,1,16,128]{3,2,1,0:T(8,128)S(1)}, f32[2,1,16,128]{3,2,1,0:T(8,128)S(1)}, u32[]{:S(2)}, u32[]{:S(2)}) collective-permute-start(f32[2,1,16,128]{3,2,1,0:T(8,128)S(1)} %slice.1424), channel_id=1, source_target_pairs={{0,2},{2,4},{4,6},{6,8},{8,10},{10,12},{12,14},{1,3},{3,5},{5,7},{... | collective-permute-start | bytes 49160 | tf_op jit(solution)/shard_map/ppermute | solution.py:14
  123.0 5.4 %collective-permute-start.16 = (f32[2,16,1,128]{3,1,2,0:T(8,128)S(1)}, f32[2,16,1,128]{3,1,2,0:T(8,128)S(1)}, u32[]{:S(2)}, u32[]{:S(2)}) collective-permute-start(f32[2,16,1,128]{3,1,2,0:T(8,128)S(1)} %bitcast.589), channel_id=1, source_target_pairs={{1,0},{3,2},{5,4},{7,6},{9,8},{11,10},{13,12},{15,14},{17,16},{19,... | collective-permute-start | bytes 49160 | tf_op jit(solution)/shard_map/ppermute | solution.py:14
  129.9 5.2 %collective-permute-done.17 = f32[2,1,16,128]{3,2,1,0:T(8,128)S(1)} collective-permute-done((f32[2,1,16,128]{3,2,1,0:T(8,128)S(1)}, f32[2,1,16,128]{3,2,1,0:T(8,128)S(1)}, u32[]{:S(2)}, u32[]{:S(2)}) %collective-permute-start.17) | collective-permute-done | bytes 16416 | tf_op jit(solution)/shard_map/ppermute | solution.py:14
  137.8 4.8 %collective-permute-start.19 = (f32[2,1,16,128]{3,2,1,0:T(8,128)S(1)}, f32[2,1,16,128]{3,2,1,0:T(8,128)S(1)}, u32[]{:S(2)}, u32[]{:S(2)}) collective-permute-start(f32[2,1,16,128]{3,2,1,0:T(8,128)S(1)} %slice.1453), channel_id=1, source_target_pairs={{0,2},{2,4},{4,6},{6,8},{8,10},{10,12},{12,14},{1,3},{3,5},{5,7},{... | collective-permute-start | bytes 49160 | tf_op jit(solution)/shard_map/ppermute | solution.py:14
  151.0 5.4 %collective-permute-start.20 = (f32[2,16,1,128]{3,1,2,0:T(8,128)S(1)}, f32[2,16,1,128]{3,1,2,0:T(8,128)S(1)}, u32[]{:S(2)}, u32[]{:S(2)}) collective-permute-start(f32[2,16,1,128]{3,1,2,0:T(8,128)S(1)} %bitcast.590), channel_id=1, source_target_pairs={{1,0},{3,2},{5,4},{7,6},{9,8},{11,10},{13,12},{15,14},{17,16},{19,... | collective-permute-start | bytes 49160 | tf_op jit(solution)/shard_map/ppermute | solution.py:14
  157.9 5.2 %collective-permute-done.21 = f32[2,1,16,128]{3,2,1,0:T(8,128)S(1)} collective-permute-done((f32[2,1,16,128]{3,2,1,0:T(8,128)S(1)}, f32[2,1,16,128]{3,2,1,0:T(8,128)S(1)}, u32[]{:S(2)}, u32[]{:S(2)}) %collective-permute-start.21) | collective-permute-done | bytes 16416 | tf_op jit(solution)/shard_map/ppermute | solution.py:14
  166.0 4.8 %collective-permute-start.23 = (f32[2,1,16,128]{3,2,1,0:T(8,128)S(1)}, f32[2,1,16,128]{3,2,1,0:T(8,128)S(1)}, u32[]{:S(2)}, u32[]{:S(2)}) collective-permute-start(f32[2,1,16,128]{3,2,1,0:T(8,128)S(1)} %slice.1486), channel_id=1, source_target_pairs={{0,2},{2,4},{4,6},{6,8},{8,10},{10,12},{12,14},{1,3},{3,5},{5,7},{... | collective-permute-start | bytes 49160 | tf_op jit(solution)/shard_map/ppermute | solution.py:14
  176.2 4.5 %scatter-add.16 = f32[3,16,16,128]{3,2,1,0:T(8,128)S(1)} dynamic-update-slice(f32[3,16,16,128]{3,2,1,0:T(8,128)S(1)} %copy.88, f32[2,16,16,1]{3,2,1,0:T(8,128)} %add_select_fusion.1, s32[]{:T(128)} %bitcast.4, s32[]{:T(128)} %constant.106.clone.1, s32[]{:T(128)} %constant.106.clone.1, s32[]{:T(128)} %bitcast.5) | dynamic-update-slice | bytes 4100 | tf_op jit(solution)/shard_map/scatter-add | solution.py:112
  180.8 5.4 %collective-permute-start.24 = (f32[2,16,1,128]{3,1,2,0:T(8,128)S(1)}, f32[2,16,1,128]{3,1,2,0:T(8,128)S(1)}, u32[]{:S(2)}, u32[]{:S(2)}) collective-permute-start(f32[2,16,1,128]{3,1,2,0:T(8,128)S(1)} %bitcast.591), channel_id=1, source_target_pairs={{1,0},{3,2},{5,4},{7,6},{9,8},{11,10},{13,12},{15,14},{17,16},{19,... | collective-permute-start | bytes 49160 | tf_op jit(solution)/shard_map/ppermute | solution.py:14
  187.9 5.0 %collective-permute-done.25 = f32[2,1,16,128]{3,2,1,0:T(8,128)S(1)} collective-permute-done((f32[2,1,16,128]{3,2,1,0:T(8,128)S(1)}, f32[2,1,16,128]{3,2,1,0:T(8,128)S(1)}, u32[]{:S(2)}, u32[]{:S(2)}) %collective-permute-start.25) | collective-permute-done | bytes 16416 | tf_op jit(solution)/shard_map/ppermute | solution.py:14
  195.9 4.8 %collective-permute-start.27 = (f32[2,1,16,128]{3,2,1,0:T(8,128)S(1)}, f32[2,1,16,128]{3,2,1,0:T(8,128)S(1)}, u32[]{:S(2)}, u32[]{:S(2)}) collective-permute-start(f32[2,1,16,128]{3,2,1,0:T(8,128)S(1)} %slice.1517), channel_id=1, source_target_pairs={{0,2},{2,4},{4,6},{6,8},{8,10},{10,12},{12,14},{1,3},{3,5},{5,7},{... | collective-permute-start | bytes 49160 | tf_op jit(solution)/shard_map/ppermute | solution.py:14
  206.3 4.5 %scatter-add.19 = f32[3,16,16,128]{3,2,1,0:T(8,128)S(1)} dynamic-update-slice(f32[3,16,16,128]{3,2,1,0:T(8,128)S(1)} %copy.89, f32[2,16,16,1]{3,2,1,0:T(8,128)} %add_select_fusion, s32[]{:T(128)} %bitcast.4, s32[]{:T(128)} %constant.106.clone.1, s32[]{:T(128)} %constant.106.clone.1, s32[]{:T(128)} %bitcast.5) | dynamic-update-slice | bytes 4100 | tf_op jit(solution)/shard_map/scatter-add | solution.py:112
  210.9 5.4 %collective-permute-start.28 = (f32[2,16,1,128]{3,2,1,0:T(1,128)S(1)}, f32[2,16,1,128]{3,2,1,0:T(1,128)S(1)}, u32[]{:S(2)}, u32[]{:S(2)}) collective-permute-start(f32[2,16,1,128]{3,2,1,0:T(1,128)S(1)} %slice.1285), channel_id=1, source_target_pairs={{1,0},{3,2},{5,4},{7,6},{9,8},{11,10},{13,12},{15,14},{17,16},{19,... | collective-permute-start | bytes 49160 | tf_op jit(solution)/shard_map/ppermute | solution.py:14
  217.8 5.2 %collective-permute-done.29 = f32[2,1,16,128]{3,2,1,0:T(8,128)S(1)} collective-permute-done((f32[2,1,16,128]{3,2,1,0:T(8,128)S(1)}, f32[2,1,16,128]{3,2,1,0:T(8,128)S(1)}, u32[]{:S(2)}, u32[]{:S(2)}) %collective-permute-start.29) | collective-permute-done | bytes 16416 | tf_op jit(solution)/shard_map/ppermute | solution.py:14
  226.1 4.8 %collective-permute-start.31 = (f32[2,1,16,128]{3,2,1,0:T(8,128)S(1)}, f32[2,1,16,128]{3,2,1,0:T(8,128)S(1)}, u32[]{:S(2)}, u32[]{:S(2)}) collective-permute-start(f32[2,1,16,128]{3,2,1,0:T(8,128)S(1)} %slice.1548), channel_id=1, source_target_pairs={{0,2},{2,4},{4,6},{6,8},{8,10},{10,12},{12,14},{1,3},{3,5},{5,7},{... | collective-permute-start | bytes 49160 | tf_op jit(solution)/shard_map/ppermute | solution.py:14
  237.9 26.3 %psum.14 = f32[]{:T(128)} all-reduce(f32[]{:T(128)S(6)} %add.231), channel_id=1, replica_groups=mesh['tx'=16,'gx'=8,'gy'=2] {'tx'}, use_global_device_ids=true, to_apply=%region_6.0 | all-reduce | flops 1 | bytes 8 | tf_op jit(solution)/shard_map/psum | solution.py:122
  264.2 41.1 %psum.15 = f32[]{:T(128)} all-reduce(f32[]{:T(128)} %psum.14), channel_id=1, replica_groups=mesh['tx'=16,'gx'=8,'gy'=2] {'gx','gy'}, use_global_device_ids=true, to_apply=%region_7.0 | all-reduce | flops 1 | bytes 8 | tf_op jit(solution)/shard_map/psum | solution.py:123
  (438 shorter events, 114.6 us)
Async XLA Ops:
  7.2 298.1 %reduce-scatter.2.cloned.1.call-start = ((), (), s32[]{:S(2)}) async-start(), calls=%async_computation.1 | async-start | bytes 278528 | tf_op jit(solution)/shard_map/reduce_scatter | solution.py:130
  8.3 13.2 %collective-permute-start = (f32[2,16,1,128]{3,2,1,0:T(1,128)S(1)}, f32[2,16,1,128]{3,2,1,0:T(1,128)S(1)}, u32[]{:S(2)}, u32[]{:S(2)}) collective-permute-start(f32[2,16,1,128]{3,2,1,0:T(1,128)S(1)} %slice.1044), channel_id=1, source_target_pairs={{1,0},{3,2},{5,4},{7,6},{9,8},{11,10},{13,12},{15,14},{17,16},{19,... | collective-permute-start | bytes 49160 | tf_op jit(solution)/shard_map/ppermute | solution.py:14
  12.3 9.2 %collective-permute-start.1 = (f32[2,1,16,128]{3,2,1,0:T(8,128)S(1)}, f32[2,1,16,128]{3,2,1,0:T(8,128)S(1)}, u32[]{:S(2)}, u32[]{:S(2)}) collective-permute-start(f32[2,1,16,128]{3,2,1,0:T(8,128)S(1)} %slice.1328), channel_id=1, source_target_pairs={{2,0},{4,2},{6,4},{8,6},{10,8},{12,10},{14,12},{3,1},{5,3},{7,5},{... | collective-permute-start | bytes 49160 | tf_op jit(solution)/shard_map/ppermute | solution.py:14
  21.8 7.1 %collective-permute-start.2 = (f32[2,16,1,128]{3,1,2,0:T(8,128)S(1)}, f32[2,16,1,128]{3,1,2,0:T(8,128)S(1)}, u32[]{:S(2)}, u32[]{:S(2)}) collective-permute-start(f32[2,16,1,128]{3,1,2,0:T(8,128)S(1)} %bitcast.592), channel_id=1, source_target_pairs={{0,1},{2,3},{4,5},{6,7},{8,9},{10,11},{12,13},{14,15},{16,17},{18,... | collective-permute-start | bytes 49160 | tf_op jit(solution)/shard_map/ppermute | solution.py:14
  31.4 10.1 %collective-permute-start.4 = (f32[2,16,1,128]{3,2,1,0:T(1,128)S(1)}, f32[2,16,1,128]{3,2,1,0:T(1,128)S(1)}, u32[]{:S(2)}, u32[]{:S(2)}) collective-permute-start(f32[2,16,1,128]{3,2,1,0:T(1,128)S(1)} %slice.1076), channel_id=1, source_target_pairs={{1,0},{3,2},{5,4},{7,6},{9,8},{11,10},{13,12},{15,14},{17,16},{19,... | collective-permute-start | bytes 49160 | tf_op jit(solution)/shard_map/ppermute | solution.py:14
  36.8 6.5 %collective-permute-start.5 = (f32[2,1,16,128]{3,2,1,0:T(8,128)S(1)}, f32[2,1,16,128]{3,2,1,0:T(8,128)S(1)}, u32[]{:S(2)}, u32[]{:S(2)}) collective-permute-start(f32[2,1,16,128]{3,2,1,0:T(8,128)S(1)} %slice.1355), channel_id=1, source_target_pairs={{2,0},{4,2},{6,4},{8,6},{10,8},{12,10},{14,12},{3,1},{5,3},{7,5},{... | collective-permute-start | bytes 49160 | tf_op jit(solution)/shard_map/ppermute | solution.py:14
  45.2 7.1 %collective-permute-start.6 = (f32[2,16,1,128]{3,1,2,0:T(8,128)S(1)}, f32[2,16,1,128]{3,1,2,0:T(8,128)S(1)}, u32[]{:S(2)}, u32[]{:S(2)}) collective-permute-start(f32[2,16,1,128]{3,1,2,0:T(8,128)S(1)} %bitcast.593), channel_id=1, source_target_pairs={{0,1},{2,3},{4,5},{6,7},{8,9},{10,11},{12,13},{14,15},{16,17},{18,... | collective-permute-start | bytes 49160 | tf_op jit(solution)/shard_map/ppermute | solution.py:14
  58.3 7.9 %collective-permute-start.8 = (f32[2,16,1,128]{3,2,1,0:T(1,128)S(1)}, f32[2,16,1,128]{3,2,1,0:T(1,128)S(1)}, u32[]{:S(2)}, u32[]{:S(2)}) collective-permute-start(f32[2,16,1,128]{3,2,1,0:T(1,128)S(1)} %copy-done.74), channel_id=1, source_target_pairs={{1,0},{3,2},{5,4},{7,6},{9,8},{11,10},{13,12},{15,14},{17,16},{19,... | collective-permute-start | bytes 49160 | tf_op jit(solution)/shard_map/ppermute | solution.py:14
  63.8 6.5 %collective-permute-start.9 = (f32[2,1,16,128]{3,2,1,0:T(8,128)S(1)}, f32[2,1,16,128]{3,2,1,0:T(8,128)S(1)}, u32[]{:S(2)}, u32[]{:S(2)}) collective-permute-start(f32[2,1,16,128]{3,2,1,0:T(8,128)S(1)} %copy-done.72), channel_id=1, source_target_pairs={{2,0},{4,2},{6,4},{8,6},{10,8},{12,10},{14,12},{3,1},{5,3},{7,5},{... | collective-permute-start | bytes 49160 | tf_op jit(solution)/shard_map/ppermute | solution.py:14
  73.6 7.1 %collective-permute-start.10 = (f32[2,16,1,128]{3,1,2,0:T(8,128)S(1)}, f32[2,16,1,128]{3,1,2,0:T(8,128)S(1)}, u32[]{:S(2)}, u32[]{:S(2)}) collective-permute-start(f32[2,16,1,128]{3,1,2,0:T(8,128)S(1)} %bitcast.594), channel_id=1, source_target_pairs={{0,1},{2,3},{4,5},{6,7},{8,9},{10,11},{12,13},{14,15},{16,17},{18,... | collective-permute-start | bytes 49160 | tf_op jit(solution)/shard_map/ppermute | solution.py:14
  88.3 9.8 %collective-permute-start.12 = (f32[2,16,1,128]{3,1,2,0:T(8,128)}, f32[2,16,1,128]{3,1,2,0:T(8,128)}, u32[]{:S(2)}, u32[]{:S(2)}) collective-permute-start(f32[2,16,1,128]{3,1,2,0:T(8,128)} %bitcast.197), channel_id=1, source_target_pairs={{1,0},{3,2},{5,4},{7,6},{9,8},{11,10},{13,12},{15,14},{17,16},{19,... | collective-permute-start | bytes 49160 | tf_op jit(solution)/shard_map/ppermute | solution.py:14
  94.5 6.6 %collective-permute-start.13 = (f32[2,1,16,128]{3,2,1,0:T(8,128)S(1)}, f32[2,1,16,128]{3,2,1,0:T(8,128)}, u32[]{:S(2)}, u32[]{:S(2)}) collective-permute-start(f32[2,1,16,128]{3,2,1,0:T(8,128)S(1)} %copy-done.73), channel_id=1, source_target_pairs={{2,0},{4,2},{6,4},{8,6},{10,8},{12,10},{14,12},{3,1},{5,3},{7,5},{... | collective-permute-start | bytes 49160 | tf_op jit(solution)/shard_map/ppermute | solution.py:14
  105.3 7.1 %collective-permute-start.14 = (f32[2,16,1,128]{3,1,2,0:T(8,128)S(1)}, f32[2,16,1,128]{3,1,2,0:T(8,128)S(1)}, u32[]{:S(2)}, u32[]{:S(2)}) collective-permute-start(f32[2,16,1,128]{3,1,2,0:T(8,128)S(1)} %bitcast.595), channel_id=1, source_target_pairs={{0,1},{2,3},{4,5},{6,7},{8,9},{10,11},{12,13},{14,15},{16,17},{18,... | collective-permute-start | bytes 49160 | tf_op jit(solution)/shard_map/ppermute | solution.py:14
  123.0 6.9 %collective-permute-start.16 = (f32[2,16,1,128]{3,1,2,0:T(8,128)S(1)}, f32[2,16,1,128]{3,1,2,0:T(8,128)S(1)}, u32[]{:S(2)}, u32[]{:S(2)}) collective-permute-start(f32[2,16,1,128]{3,1,2,0:T(8,128)S(1)} %bitcast.589), channel_id=1, source_target_pairs={{1,0},{3,2},{5,4},{7,6},{9,8},{11,10},{13,12},{15,14},{17,16},{19,... | collective-permute-start | bytes 49160 | tf_op jit(solution)/shard_map/ppermute | solution.py:14
  128.5 6.5 %collective-permute-start.17 = (f32[2,1,16,128]{3,2,1,0:T(8,128)S(1)}, f32[2,1,16,128]{3,2,1,0:T(8,128)S(1)}, u32[]{:S(2)}, u32[]{:S(2)}) collective-permute-start(f32[2,1,16,128]{3,2,1,0:T(8,128)S(1)} %slice.1440), channel_id=1, source_target_pairs={{2,0},{4,2},{6,4},{8,6},{10,8},{12,10},{14,12},{3,1},{5,3},{7,5},{... | collective-permute-start | bytes 49160 | tf_op jit(solution)/shard_map/ppermute | solution.py:14
  136.4 7.1 %collective-permute-start.18 = (f32[2,16,1,128]{3,1,2,0:T(8,128)S(1)}, f32[2,16,1,128]{3,1,2,0:T(8,128)S(1)}, u32[]{:S(2)}, u32[]{:S(2)}) collective-permute-start(f32[2,16,1,128]{3,1,2,0:T(8,128)S(1)} %bitcast.596), channel_id=1, source_target_pairs={{0,1},{2,3},{4,5},{6,7},{8,9},{10,11},{12,13},{14,15},{16,17},{18,... | collective-permute-start | bytes 49160 | tf_op jit(solution)/shard_map/ppermute | solution.py:14
  151.0 6.9 %collective-permute-start.20 = (f32[2,16,1,128]{3,1,2,0:T(8,128)S(1)}, f32[2,16,1,128]{3,1,2,0:T(8,128)S(1)}, u32[]{:S(2)}, u32[]{:S(2)}) collective-permute-start(f32[2,16,1,128]{3,1,2,0:T(8,128)S(1)} %bitcast.590), channel_id=1, source_target_pairs={{1,0},{3,2},{5,4},{7,6},{9,8},{11,10},{13,12},{15,14},{17,16},{19,... | collective-permute-start | bytes 49160 | tf_op jit(solution)/shard_map/ppermute | solution.py:14
  156.6 6.5 %collective-permute-start.21 = (f32[2,1,16,128]{3,2,1,0:T(8,128)S(1)}, f32[2,1,16,128]{3,2,1,0:T(8,128)S(1)}, u32[]{:S(2)}, u32[]{:S(2)}) collective-permute-start(f32[2,1,16,128]{3,2,1,0:T(8,128)S(1)} %slice.1473), channel_id=1, source_target_pairs={{2,0},{4,2},{6,4},{8,6},{10,8},{12,10},{14,12},{3,1},{5,3},{7,5},{... | collective-permute-start | bytes 49160 | tf_op jit(solution)/shard_map/ppermute | solution.py:14
  164.6 7.1 %collective-permute-start.22 = (f32[2,16,1,128]{3,1,2,0:T(8,128)S(1)}, f32[2,16,1,128]{3,1,2,0:T(8,128)S(1)}, u32[]{:S(2)}, u32[]{:S(2)}) collective-permute-start(f32[2,16,1,128]{3,1,2,0:T(8,128)S(1)} %bitcast.597), channel_id=1, source_target_pairs={{0,1},{2,3},{4,5},{6,7},{8,9},{10,11},{12,13},{14,15},{16,17},{18,... | collective-permute-start | bytes 49160 | tf_op jit(solution)/shard_map/ppermute | solution.py:14
  180.8 7.1 %collective-permute-start.24 = (f32[2,16,1,128]{3,1,2,0:T(8,128)S(1)}, f32[2,16,1,128]{3,1,2,0:T(8,128)S(1)}, u32[]{:S(2)}, u32[]{:S(2)}) collective-permute-start(f32[2,16,1,128]{3,1,2,0:T(8,128)S(1)} %bitcast.591), channel_id=1, source_target_pairs={{1,0},{3,2},{5,4},{7,6},{9,8},{11,10},{13,12},{15,14},{17,16},{19,... | collective-permute-start | bytes 49160 | tf_op jit(solution)/shard_map/ppermute | solution.py:14
  186.4 6.5 %collective-permute-start.25 = (f32[2,1,16,128]{3,2,1,0:T(8,128)S(1)}, f32[2,1,16,128]{3,2,1,0:T(8,128)S(1)}, u32[]{:S(2)}, u32[]{:S(2)}) collective-permute-start(f32[2,1,16,128]{3,2,1,0:T(8,128)S(1)} %slice.1504), channel_id=1, source_target_pairs={{2,0},{4,2},{6,4},{8,6},{10,8},{12,10},{14,12},{3,1},{5,3},{7,5},{... | collective-permute-start | bytes 49160 | tf_op jit(solution)/shard_map/ppermute | solution.py:14
  194.6 7.1 %collective-permute-start.26 = (f32[2,16,1,128]{3,1,2,0:T(8,128)S(1)}, f32[2,16,1,128]{3,1,2,0:T(8,128)S(1)}, u32[]{:S(2)}, u32[]{:S(2)}) collective-permute-start(f32[2,16,1,128]{3,1,2,0:T(8,128)S(1)} %bitcast.598), channel_id=1, source_target_pairs={{0,1},{2,3},{4,5},{6,7},{8,9},{10,11},{12,13},{14,15},{16,17},{18,... | collective-permute-start | bytes 49160 | tf_op jit(solution)/shard_map/ppermute | solution.py:14
  210.9 6.9 %collective-permute-start.28 = (f32[2,16,1,128]{3,2,1,0:T(1,128)S(1)}, f32[2,16,1,128]{3,2,1,0:T(1,128)S(1)}, u32[]{:S(2)}, u32[]{:S(2)}) collective-permute-start(f32[2,16,1,128]{3,2,1,0:T(1,128)S(1)} %slice.1285), channel_id=1, source_target_pairs={{1,0},{3,2},{5,4},{7,6},{9,8},{11,10},{13,12},{15,14},{17,16},{19,... | collective-permute-start | bytes 49160 | tf_op jit(solution)/shard_map/ppermute | solution.py:14
  224.7 7.1 %collective-permute-start.30 = (f32[2,16,1,128]{3,1,2,0:T(8,128)S(1)}, f32[2,16,1,128]{3,1,2,0:T(8,128)S(1)}, u32[]{:S(2)}, u32[]{:S(2)}) collective-permute-start(f32[2,16,1,128]{3,1,2,0:T(8,128)S(1)} %bitcast.599), channel_id=1, source_target_pairs={{0,1},{2,3},{4,5},{6,7},{8,9},{10,11},{12,13},{14,15},{16,17},{18,... | collective-permute-start | bytes 49160 | tf_op jit(solution)/shard_map/ppermute | solution.py:14
  (91 other events, 190.2 us)
Sparse Core Ops, SparseCore 0:
  235.6 61.6 reduce-scatter.1
